TPU v7x, 256 devices: a whole 4x4x8 slice. The times are simulated.
256 devices in a mesh: req: 4 (over x_hi, core), tp: 64 (over z, x_lo, y).
Axes of the slice: x: 4 (x_hi: 2, x_lo: 2; x = x_hi * 2 + x_lo), y: 4, z: 8, core: 2. Of those that a mesh axis runs over, the one named last changes fastest.
Arguments:
- hidden: bfloat16 [4096, 8192], P('req', 'tp'), may hold values from -6 to 6
- query_weight: bfloat16 [8192, 8192], P(None, 'tp'), may hold values from -0.0625 to 0.0625
- key_value_weight: bfloat16 [8192, 2048], P(None, 'tp'), may hold values from -0.0625 to 0.0625
- adapter_down_maps: bfloat16 [64, 8192, 32], P('req', 'tp'), may hold values from -0.0625 to 0.0625
- adapter_up_maps: bfloat16 [64, 32, 8192], P('req', None, 'tp'), may hold values from -1 to 1
- token_request_start: int32 [4096], P('req'), may hold values from 0 to 31, as said below
- adapter_per_block: int32 [32], P('req'), may hold values from 0 to 63
Outputs:
- context: bfloat16 [4096, 8192], P('req', 'tp')
Inputs may be any that keep to these rules, and one draw needn't show every extreme that they name: `token_request_start`: each run of 1024 tokens along the req split holds whole requests; a request is a run of whole blocks of 128 tokens; the last block of each such run is a request of its own.
All inputs are finite; a program needn't handle non-finite values.
Results may differ from a plain program's by a relative error of at most 0.012.
Values may be sent and summed in bfloat16 or wider, within the bound.
No kernel may reach another device: no remote copies, remote signals or barrier semaphores. Data moves between devices by JAX's collectives and lax.ppermute only.
A program may use at most 64 MiB of HBM per device.

v0:
```python
import math
import jax
import jax.numpy as jnp
from jax import lax
from jax.sharding import PartitionSpec as P

HEAD_SIZE = 128
BLOCK = 128
ROPE_BASE = 500000.0
ADAPTER_SCALE = 2.0


def from_partner(block, axis, bit):
    count = lax.axis_size(axis)
    route = []
    for low in range(count):
        high = low | 1 << bit
        if high != low and high < count:
            route += [(low, high), (high, low)]
    return lax.ppermute(block, axis, route)


def rotate(vectors, positions):
    half_width = vectors.shape[-1] // 2
    steps_half = jnp.arange(half_width, dtype=jnp.float32)
    inverse = jnp.exp(-(2.0 * steps_half / vectors.shape[-1]) * math.log(ROPE_BASE))
    angles = positions.astype(jnp.float32)[:, None] * inverse[None, :]
    cosines = jnp.cos(angles)
    sines = jnp.sin(angles)
    front_half = vectors[:, :half_width]
    back_half = vectors[:, half_width:]
    return jnp.concatenate(
        [front_half * cosines - back_half * sines, back_half * cosines + front_half * sines], axis=1
    )


def attend(queries, key_rows, value_rows, request):
    group_rows = queries.shape[0]
    block_rows = min(512, group_rows)
    block_total = group_rows // block_rows
    places = jnp.arange(group_rows, dtype=jnp.int32)
    score_scale = 1.0 / math.sqrt(queries.shape[1])

    def one_block(block_index):
        begin_row = block_index * block_rows
        q_blk = lax.dynamic_slice_in_dim(queries, begin_row, block_rows, 0)
        r_blk = lax.dynamic_slice_in_dim(request, begin_row, block_rows, 0)
        p_blk = lax.dynamic_slice_in_dim(places, begin_row, block_rows, 0)
        scores = (
            lax.dot_general(
                q_blk, key_rows, (((1,), (1,)), ((), ())), preferred_element_type=jnp.float32
            )
            * score_scale
        )
        allowed = (r_blk[:, None] == request[None, :]) & (places[None, :] <= p_blk[:, None])
        scores = jnp.where(allowed, scores, jnp.float32(-1e30))
        row_max = jnp.max(scores, axis=1, keepdims=True)
        weights = jnp.exp(scores - row_max)
        probs = (weights / jnp.sum(weights, axis=1, keepdims=True)).astype(jnp.bfloat16)
        return jnp.dot(probs, value_rows, preferred_element_type=jnp.float32).astype(jnp.bfloat16)

    blocks = lax.map(one_block, jnp.arange(block_total, dtype=jnp.int32))
    return blocks.reshape(group_rows, value_rows.shape[1])


def body(
    hidden,
    query_weight,
    key_value_weight,
    adapter_down_maps,
    adapter_up_maps,
    token_request_start,
    adapter_per_block,
):
    group_rows = hidden.shape[0]
    local_width = hidden.shape[1]
    head_cols = query_weight.shape[1]
    kv_cols = key_value_weight.shape[1]
    device = lax.axis_index("tp")
    spread = 2 * HEAD_SIZE // kv_cols
    piece = lax.all_gather(hidden, "tp", axis=1, tiled=True)
    query_total = jnp.dot(piece, query_weight, preferred_element_type=jnp.float32)
    kv_sum = jnp.dot(piece, key_value_weight, preferred_element_type=jnp.float32)
    down_all, up_all = (
        lax.all_gather(adapter_down_maps, "req", axis=0, tiled=True),
        lax.all_gather(adapter_up_maps, "req", axis=0, tiled=True),
    )
    block_total = group_rows // BLOCK
    chosen_down = down_all[adapter_per_block]
    chosen_up = up_all[adapter_per_block]
    block_grouped = hidden.reshape(block_total, BLOCK, local_width)
    reduced_part = jnp.einsum(
        "uqo,uop->uqp", block_grouped, chosen_down, preferred_element_type=jnp.float32
    )
    reduced_rank = lax.psum(reduced_part, "tp").astype(jnp.bfloat16)
    adapter_term = jnp.einsum(
        "epl,elm->epm", reduced_rank, chosen_up, preferred_element_type=jnp.float32
    ).reshape(group_rows, head_cols)
    places = lax.axis_index("req") * group_rows + jnp.arange(group_rows, dtype=jnp.int32)
    positions = places - token_request_start * BLOCK
    complete_query = query_total + ADAPTER_SCALE * adapter_term
    kv_piece = kv_sum.astype(jnp.bfloat16)
    head_block = kv_piece
    for bit_number in range(spread.bit_length() - 1):
        partner = from_partner(head_block, "tp", bit_number)
        upper_side = device // 2**bit_number % 2
        head_block = jnp.where(
            upper_side == 1,
            jnp.concatenate([partner, head_block], axis=1),
            jnp.concatenate([head_block, partner], axis=1),
        )
    key_rows = rotate(head_block[:, :HEAD_SIZE].astype(jnp.float32), positions).astype(jnp.bfloat16)
    value_rows = head_block[:, HEAD_SIZE:]
    head_query = rotate(complete_query, positions).astype(jnp.bfloat16)
    outputs = attend(head_query, key_rows, value_rows, token_request_start)
    return outputs


def solution(mesh):
    in_specs = (
        P("req", "tp"),
        P(None, "tp"),
        P(None, "tp"),
        P("req", "tp", None),
        P("req", None, "tp"),
        P("req"),
        P("req"),
    )
    out_specs = P("req", "tp")
    return jax.shard_map(body, mesh=mesh, in_specs=in_specs, out_specs=out_specs, check_vma=False)
```

profile of v0, /device:TPU:4, one launch (start us, length us, event | category | flops | bytes accessed | tf_op | source)
XLA Modules:
  0.0 415.5 jit_solution(10693275927732517615)
XLA Ops:
  6.5 0.0 copy-start
  6.5 0.0 copy-start.1
  6.5 0.0 all-gather.2.cloned.1.call-start
  6.5 0.7 all-gather.2.cloned.1.call-update
  7.3 0.7 compare_select_fusion
  8.0 8.5 %all_gather.10 = bf16[64,128,32]{1,2,0:T(8,128)(2,1)S(1)} all-gather(bf16[16,128,32]{1,2,0:T(8,128)(2,1)} %param.12), channel_id=1, replica_groups=mesh['req'=4,'tp'=64] {'req'}, dimensions={0}, use_global_device_ids=true | all-gather | bytes 655360 | tf_op jit(solution)/shard_map/all_gather | solution.py:85
  16.5 0.6 gather_fusion
  17.0 1.2 convolution_bitcast_fusion
  18.2 11.8 %all_gather.11 = bf16[64,32,128]{2,1,0:T(8,128)(2,1)S(1)} all-gather(bf16[16,32,128]{2,1,0:T(8,128)(2,1)} %param.13), channel_id=1, replica_groups=mesh['req'=4,'tp'=64] {'req'}, dimensions={0}, use_global_device_ids=true | all-gather | bytes 655360 | tf_op jit(solution)/shard_map/all_gather | solution.py:86
  30.0 0.6 gather_fusion.1
  30.6 314.2 %all-reduce.1 = bf16[8,128,32]{1,2,0:T(8,128)(2,1)S(1)} all-reduce(f32[8,128,32]{1,2,0:T(8,128)S(1)} %convolution_bitcast_fusion), channel_id=1, replica_groups=mesh['req'=4,'tp'=64] {'tp'}, use_global_device_ids=true, to_apply=%region_0.0 | all-reduce | flops 32768 | bytes 196608 | tf_op jit(solution)/shard_map/psum | solution.py:95
  344.8 13.7 %all-gather.2.cloned.1.call-done = bf16[1024,8192]{1,0:T(8,128)(2,1)} async-done(((bf16[1024,128]{1,0:T(8,128)(2,1)}), bf16[1024,8192]{1,0:T(8,128)(2,1)}) %all-gather.2.cloned.1.call-update) | async-done | bytes 16777232 | tf_op jit(solution)/shard_map/all_gather | solution.py:81
  358.5 0.0 copy-done.1
  358.5 10.8 %convolution_convert_fusion.1 = bf16[1024,32]{0,1:T(8,128)(2,1)S(1)} fusion(bf16[1024,8192]{1,0:T(8,128)(2,1)} %all-gather.2.cloned.1.call-done, bf16[8192,32]{0,1:T(8,128)(2,1)S(1)} %copy-done.1), kind=kOutput, calls=%fused_computation.14 | convolution fusion | flops 536903680 | bytes 17367040 | tf_op jit(solution)/shard_map/dot_general | solution.py:83
  369.3 0.5 collective-permute-start
  369.9 0.3 convolution_multiply_fusion
  370.2 3.5 collective-permute-done
  373.7 6.2 %collective-permute-start.1 = (bf16[1024,64]{0,1:T(8,128)(2,1)S(1)}, bf16[1024,64]{0,1:T(8,128)(2,1)}, u32[]{:S(2)}, u32[]{:S(2)}) collective-permute-start(bf16[1024,64]{0,1:T(8,128)(2,1)S(1)} %maximum_select_fusion.2), channel_id=1, source_target_pairs={{0,2},{2,0},{1,3},{3,1},{4,6},{6,4},{5,7},{7,5},{8,10},{10,8},{9,1... | collective-permute-start | bytes 393224 | tf_op jit(solution)/shard_map/ppermute | solution.py:20
  379.8 0.0 copy-done.2
  379.8 0.2 copy.16
  380.0 2.8 collective-permute-done.1
  382.9 1.0 maximum_select_fusion.1
  383.9 3.0 collective-permute-start.2
  386.9 0.0 copy-done
  386.9 11.4 %convolution_add_fusion = f32[1024,128]{0,1:T(8,128)S(1)} fusion(f32[1024,128]{0,1:T(8,128)S(1)} %copy.16, bf16[1024,8192]{1,0:T(8,128)(2,1)} %all-gather.2.cloned.1.call-done, bf16[8192,128]{1,0:T(8,128)(2,1)S(1)} %copy-done), kind=kOutput, calls=%fused_computation.12 | convolution fusion | flops 2147614720 | bytes 19922944 | tf_op jit(solution)/shard_map/dot_general | solution.py:82
  398.3 0.0 collective-permute-done.2
  398.3 1.2 maximum_select_fusion
  399.6 0.1 fusion.23
  399.6 0.0 copy-start.3
  399.6 1.2 fusion.18
  400.9 0.2 copy.14
  401.1 0.2 copy.15
  401.3 0.0 copy-done.3
  401.3 6.7 %while.11 = (s32[]{:T(128)}, bf16[2,512,128]{2,1,0:T(8,128)(2,1)S(1)}, s32[2]{0:T(128)S(1)}, s32[1024]{0:T(1024)S(1)}, s32[1024]{0:T(1024)S(1)}, /*index=5*/bf16...) while((s32[]{:T(128)}, ...), condition=%wide.region_4.5_spmd.clone, body=%wide.region_1.4_spmd.clone.sunk | while | flops 274267136 | bytes 7108799 | solution.py:62
  401.3 0.6 dynamic_slice.26
  402.5 0.1 dynamic_slice.27
  402.6 0.1 dynamic_slice.28
  402.7 0.8 fusion.41
  403.5 0.5 fusion.42
  404.0 0.6 fusion.43
  404.6 0.6 dynamic_slice.26
  405.9 0.1 dynamic_slice.27
  406.0 0.1 dynamic_slice.28
  406.0 0.8 fusion.41
  406.8 0.5 fusion.42
  407.3 0.6 fusion.43
  408.0 0.0 copy-start.4
  408.0 0.7 copy-done.4
  (9 shorter events, 0.1 us)
Async XLA Ops:
  6.5 380.4 %copy-start = (bf16[8192,128]{1,0:T(8,128)(2,1)S(1)}, bf16[8192,128]{1,0:T(8,128)(2,1)}, u32[]{:S(2)}) copy-start(bf16[8192,128]{1,0:T(8,128)(2,1)} %param.10) | copy-start | bytes 6291460
  6.5 352.0 %copy-start.1 = (bf16[8192,32]{0,1:T(8,128)(2,1)S(1)}, bf16[8192,32]{0,1:T(8,128)(2,1)}, u32[]{:S(2)}) copy-start(bf16[8192,32]{0,1:T(8,128)(2,1)} %param.11) | copy-start | bytes 1572868
  6.5 352.0 %all-gather.2.cloned.1.call-start = ((), (), s32[]{:S(2)}) async-start(), calls=%async_computation | async-start | bytes 17039360 | tf_op jit(solution)/shard_map/all_gather | solution.py:81
  344.8 35.0 %copy-start.2 = (s32[1024]{0:T(1024)S(1)}, s32[1024]{0:T(1024)}, u32[]{:S(2)}) copy-start(s32[1024]{0:T(1024)} %param.14) | copy-start | bytes 12292
  369.3 4.3 %collective-permute-start = (bf16[1024,32]{0,1:T(8,128)(2,1)S(1)}, bf16[1024,32]{0,1:T(8,128)(2,1)S(1)}, u32[]{:S(2)}, u32[]{:S(2)}) collective-permute-start(bf16[1024,32]{0,1:T(8,128)(2,1)S(1)} %convolution_convert_fusion.1), channel_id=1, source_target_pairs={{0,1},{1,0},{2,3},{3,2},{4,5},{5,4},{6,7},{7,6},{8,9},{9,8},{10,11... | collective-permute-start | bytes 196616 | tf_op jit(solution)/shard_map/ppermute | solution.py:20
  373.7 9.2 %collective-permute-start.1 = (bf16[1024,64]{0,1:T(8,128)(2,1)S(1)}, bf16[1024,64]{0,1:T(8,128)(2,1)}, u32[]{:S(2)}, u32[]{:S(2)}) collective-permute-start(bf16[1024,64]{0,1:T(8,128)(2,1)S(1)} %maximum_select_fusion.2), channel_id=1, source_target_pairs={{0,2},{2,0},{1,3},{3,1},{4,6},{6,4},{5,7},{7,5},{8,10},{10,8},{9,1... | collective-permute-start | bytes 393224 | tf_op jit(solution)/shard_map/ppermute | solution.py:20
  383.9 14.4 %collective-permute-start.2 = (bf16[1024,128]{0,1:T(8,128)(2,1)S(1)}, bf16[1024,128]{0,1:T(8,128)(2,1)}, u32[]{:S(2)}, u32[]{:S(2)}) collective-permute-start(bf16[1024,128]{0,1:T(8,128)(2,1)S(1)} %maximum_select_fusion.1), channel_id=1, source_target_pairs={{0,4},{4,0},{1,5},{5,1},{2,6},{6,2},{3,7},{7,3},{8,12},{12,8},{9,1... | collective-permute-start | bytes 786440 | tf_op jit(solution)/shard_map/ppermute | solution.py:20
  399.6 1.7 copy-start.3
  408.0 0.7 copy-start.4
Sparse Core Ops, SparseCore 0:
  9.1 349.3 all-gather.1
where the time goes:
time: 416 us
  blocking collectives  335 us (81%)
  matrix products  26.5 us (6%)
  waiting for transfers between devices  20.7 us (5%)
  between operations  13.6 us (3%)
  starting transfers between devices  9.68 us (2%)
  other arithmetic  5.36 us (1%)
    psum x1, blocking collectives, body(): reduced_rank = lax.psum(reduced_part, 'tp').astype(jnp.bfloat16)  314 us
    all_gather x1, waiting for transfers between devices, body(): piece = lax.all_gather(hidden, 'tp', axis=1, tiled=True)  13.7 us
    all_gather x1, blocking collectives, body(): lax.all_gather(adapter_up_maps, 'req', axis=0, tiled=True)  11.8 us
    dot_general x1, matrix products, body(): jnp.dot(piece, query_weight, preferred_element_type=jnp.float32)  11.4 us
    dot_general x1, matrix products, body(): jnp.dot(piece, key_value_weight, preferred_element_type=jnp.float32)  10.8 us
    ppermute x3, starting transfers between devices, from_partner(): return lax.ppermute(block, axis, route)  9.68 us
    all_gather x1, blocking collectives, body(): lax.all_gather(adapter_down_maps, 'req', axis=0, tiled=True)  8.48 us
  transfers between devices with their start and end apart: 4, of which 3 were waited for; matrix products, arithmetic and copies ran while one was open for 4% of the time, Pallas kernels for 0%

commit v1 on v0

--- a/solution.py
+++ b/solution.py
@@ -92,7 +92,7 @@
     reduced_part = jnp.einsum(
         "uqo,uop->uqp", block_grouped, chosen_down, preferred_element_type=jnp.float32
     )
-    reduced_rank = lax.psum(reduced_part, "tp").astype(jnp.bfloat16)
+    reduced_rank = jnp.sum(lax.all_gather(reduced_part, "tp"), axis=0).astype(jnp.bfloat16)
     adapter_term = jnp.einsum(
         "epl,elm->epm", reduced_rank, chosen_up, preferred_element_type=jnp.float32
     ).reshape(group_rows, head_cols)

time: 416 us -> 711 us (1.71)
  waiting for transfers between devices: 20.7 us -> 632 us
  blocking collectives: 335 us -> 20.1 us
  starting transfers between devices: 9.68 us -> 2.2 us
    psum x1 -> x0, blocking collectives: 314 us -> none  [body(): reduced_rank = lax.psum(reduced_part, 'tp').astype(jnp.bfloat16)]
    all_gather x1, waiting for transfers between devices: 13.7 us -> 326 us  [body(): piece = lax.all_gather(hidden, 'tp', axis=1, tiled=True)]
    all_gather x0 -> x1, waiting for transfers between devices: none -> 301 us  [body(): lax.all_gather(reduced_part, 'tp')]
    ppermute x3, starting transfers between devices: 9.68 us -> 2.13 us  [from_partner(): return lax.ppermute(block, axis, route)]
  transfers between devices with their start and end apart: 4 -> 5, of which waited for: 3 -> 3; matrix products, arithmetic and copies ran while one was open for 4% -> 4% of each run, Pallas kernels for 0% -> 0%
where the time goes in v1:
time: 711 us; the launch traced here: 710 us
  waiting for transfers between devices  632 us (89%)
  matrix products  27.2 us (4%)
  blocking collectives  20.1 us (3%)
  between operations  13.7 us (2%)
  other arithmetic  9.43 us (1%)
    all_gather x1, waiting for transfers between devices, body(): piece = lax.all_gather(hidden, 'tp', axis=1, tiled=True)  326 us
    all_gather x1, waiting for transfers between devices, body(): lax.all_gather(reduced_part, 'tp')  301 us
  transfers between devices with their start and end apart: 5, of which 3 were waited for; matrix products, arithmetic and copies ran while one was open for 4% of the time, Pallas kernels for 0%

profile of v1, /device:TPU:4, one launch (start us, length us, event | category | flops | bytes accessed | tf_op | source)
XLA Modules:
  0.0 709.9 jit_solution(9883481615692128674)
XLA Ops:
  6.5 0.0 copy-start
  6.5 0.0 all-gather.4.cloned.1.call-start
  6.6 0.7 all-gather.4.cloned.1.call-update
  7.3 0.0 all-gather.6.cloned.1.call-start
  7.3 0.7 compare_select_fusion
  8.0 8.5 %all_gather.16 = bf16[64,128,32]{1,2,0:T(8,128)(2,1)S(1)} all-gather(bf16[16,128,32]{1,2,0:T(8,128)(2,1)} %param.12), channel_id=1, replica_groups=mesh['req'=4,'tp'=64] {'req'}, dimensions={0}, use_global_device_ids=true | all-gather | bytes 655360 | tf_op jit(solution)/shard_map/all_gather | solution.py:85
  16.5 0.6 gather_fusion
  17.1 1.9 convolution_bitcast_fusion
  18.9 0.0 all-gather.6.cloned.1.call-update
  19.0 0.0 copy-done.2
  19.1 11.6 %all_gather.19 = bf16[64,32,128]{2,1,0:T(8,128)(2,1)S(1)} all-gather(bf16[16,32,128]{2,1,0:T(8,128)(2,1)S(1)} %copy-done.2), channel_id=1, replica_groups=mesh['req'=4,'tp'=64] {'req'}, dimensions={0}, use_global_device_ids=true | all-gather | bytes 655360 | tf_op jit(solution)/shard_map/all_gather | solution.py:86
  30.7 0.6 gather_fusion.1
  31.3 326.4 %all-gather.4.cloned.1.call-done = bf16[1024,8192]{1,0:T(8,128)(2,1)} async-done(((bf16[1024,128]{1,0:T(8,128)(2,1)}), bf16[1024,8192]{1,0:T(8,128)(2,1)}) %all-gather.4.cloned.1.call-update) | async-done | bytes 16777232 | tf_op jit(solution)/shard_map/all_gather | solution.py:81
  357.7 10.8 %convolution_convert_fusion.1 = bf16[1024,32]{0,1:T(8,128)(2,1)S(1)} fusion(bf16[1024,8192]{1,0:T(8,128)(2,1)} %all-gather.4.cloned.1.call-done, bf16[8192,32]{0,1:T(8,128)(2,1)S(1)} %copy-done.1), kind=kOutput, calls=%fused_computation.14 | convolution fusion | flops 536903680 | bytes 17367040 | tf_op jit(solution)/shard_map/dot_general | solution.py:83
  368.5 0.1 collective-permute-start
  368.6 300.6 %all-gather.6.cloned.1.call-done = f32[512,128,32]{1,2,0:T(8,128)} async-done(((f32[8,128,32]{1,2,0:T(8,128)}), f32[512,128,32]{1,2,0:T(8,128)}) %all-gather.6.cloned.1.call-update) | async-done | bytes 8388624 | tf_op jit(solution)/shard_map/all_gather | solution.py:95
  669.2 4.1 reduce_sum.18
  673.2 0.0 collective-permute-done
  673.3 1.8 collective-permute-start.1
  675.1 0.3 convolution_multiply_fusion
  675.4 0.2 copy.16
  675.6 4.4 collective-permute-done.1
  680.0 1.0 maximum_select_fusion.1
  681.0 0.3 collective-permute-start.2
  681.3 11.4 %convolution_add_fusion = f32[1024,128]{0,1:T(8,128)S(1)} fusion(f32[1024,128]{0,1:T(8,128)S(1)} %copy.16, bf16[1024,8192]{1,0:T(8,128)(2,1)} %all-gather.4.cloned.1.call-done, bf16[8192,128]{1,0:T(8,128)(2,1)S(1)} %copy-done), kind=kOutput, calls=%fused_computation.12 | convolution fusion | flops 2147614720 | bytes 19922944 | tf_op jit(solution)/shard_map/dot_general | solution.py:82
  692.7 0.0 collective-permute-done.2
  692.7 1.2 maximum_select_fusion
  694.0 0.1 fusion.23
  694.0 0.0 copy-start.4
  694.0 1.2 fusion.18
  695.3 0.2 copy.14
  695.5 0.2 copy.15
  695.7 0.0 copy-done.4
  695.7 6.7 while.11
  695.7 0.6 dynamic_slice.26
  697.0 0.1 dynamic_slice.27
  697.0 0.1 dynamic_slice.28
  697.1 0.8 fusion.41
  697.9 0.5 fusion.42
  698.4 0.6 fusion.43
  699.0 0.6 dynamic_slice.26
  700.3 0.1 dynamic_slice.27
  700.4 0.1 dynamic_slice.28
  700.4 0.8 fusion.41
  701.2 0.5 fusion.42
  701.7 0.6 fusion.43
  702.4 0.0 copy-start.5
  702.4 0.7 copy-done.5
  (14 shorter events, 0.1 us)
Async XLA Ops:
  6.5 674.8 %copy-start = (bf16[8192,128]{1,0:T(8,128)(2,1)S(1)}, bf16[8192,128]{1,0:T(8,128)(2,1)}, u32[]{:S(2)}) copy-start(bf16[8192,128]{1,0:T(8,128)(2,1)} %param.10) | copy-start | bytes 6291460
  6.5 12.5 %copy-start.2 = (bf16[16,32,128]{2,1,0:T(8,128)(2,1)S(1)}, bf16[16,32,128]{2,1,0:T(8,128)(2,1)}, u32[]{:S(2)}) copy-start(bf16[16,32,128]{2,1,0:T(8,128)(2,1)} %param.13) | copy-start | bytes 393220
  6.5 24.7 %copy-start.3 = (s32[1024]{0:T(1024)S(1)}, s32[1024]{0:T(1024)}, u32[]{:S(2)}) copy-start(s32[1024]{0:T(1024)} %param.14) | copy-start | bytes 12292
  6.5 351.1 %copy-start.1 = (bf16[8192,32]{0,1:T(8,128)(2,1)S(1)}, bf16[8192,32]{0,1:T(8,128)(2,1)}, u32[]{:S(2)}) copy-start(bf16[8192,32]{0,1:T(8,128)(2,1)} %param.11) | copy-start | bytes 1572868
  6.5 351.1 %all-gather.4.cloned.1.call-start = ((), (), s32[]{:S(2)}) async-start(), calls=%async_computation | async-start | bytes 17039360 | tf_op jit(solution)/shard_map/all_gather | solution.py:81
  7.3 661.9 %all-gather.6.cloned.1.call-start = ((), (), s32[]{:S(2)}) async-start(), calls=%async_computation.1 | async-start | bytes 8519680 | tf_op jit(solution)/shard_map/all_gather | solution.py:95
  368.5 304.8 %collective-permute-start = (bf16[1024,32]{0,1:T(8,128)(2,1)S(1)}, bf16[1024,32]{0,1:T(8,128)(2,1)S(1)}, u32[]{:S(2)}, u32[]{:S(2)}) collective-permute-start(bf16[1024,32]{0,1:T(8,128)(2,1)S(1)} %convolution_convert_fusion.1), channel_id=1, source_target_pairs={{0,1},{1,0},{2,3},{3,2},{4,5},{5,4},{6,7},{7,6},{8,9},{9,8},{10,11... | collective-permute-start | bytes 196616 | tf_op jit(solution)/shard_map/ppermute | solution.py:20
  673.3 6.7 collective-permute-start.1
  681.0 11.7 %collective-permute-start.2 = (bf16[1024,128]{0,1:T(8,128)(2,1)S(1)}, bf16[1024,128]{0,1:T(8,128)(2,1)}, u32[]{:S(2)}, u32[]{:S(2)}) collective-permute-start(bf16[1024,128]{0,1:T(8,128)(2,1)S(1)} %maximum_select_fusion.1), channel_id=1, source_target_pairs={{0,4},{4,0},{1,5},{5,1},{2,6},{6,2},{3,7},{7,3},{8,12},{12,8},{9,1... | collective-permute-start | bytes 786440 | tf_op jit(solution)/shard_map/ppermute | solution.py:20
  694.0 1.7 copy-start.4
  702.4 0.7 copy-start.5
Sparse Core Ops, SparseCore 0:
  9.1 348.5 all-gather.3
  359.5 309.6 all-gather.5
